TPU v7x, 32 devices: a whole 2x2x4 slice. The times are simulated.
32 devices in a mesh: groups: 2 (over y), seq: 2 (over x), frame: 4 (over z), cfg: 2 (over core).
Axes of the slice: x: 2, y: 2, z: 4, core: 2. Of those that a mesh axis runs over, the one named last changes fastest.
Arguments:
- qkv: bfloat16 [2, 4096, 3, 4096], P('cfg', ('groups', 'frame', 'seq')), parts along dimension 1, may hold values from -108 to 108, as said below
- timestep: int32 [2], P('groups'), parts along dimension 0, may hold values from 0 to 999
- windows: int32 [32], replicated, may hold values from 0 to 2
- segments: int32 [16], P('groups'), parts along dimension 0, may hold values from 0 to 3, never falling along the last dimension, each value on 1 to 4 neighbouring positions
Outputs:
- guided: bfloat16 [4096, 16, 256], P(('groups', 'frame', 'seq'), 'cfg'), parts along dimension 0
There are 2 independent parts, one for each index of `groups`. A program takes and returns all parts, laid end to end along the dimension named above; an argument that names none is the same for every part. Nothing has to cross between parts.
Inputs may be any that keep to these rules, and one draw needn't show every extreme that they name: Entries of qkv lie in this range. `segments`: shot numbers never fall from one frame to the next.
All inputs are finite; a program needn't handle non-finite values.
Results may differ from a plain program's by a relative error of at most 0.0053.
Values may be sent and summed in bfloat16 or wider, within the bound.
A program may use at most 128 MiB of HBM per device.

v0:
```python
import math

import jax
import jax.numpy as jnp
from jax import lax
from jax.sharding import PartitionSpec as P

HD = 128
F_DEV = 2
W_MAX = 2


def padded_2(block, sides, width):
    for axis, dim in sides:
        count = lax.axis_size(axis)
        forward = [(i, i + 1) for i in range(count - 1)]
        backward = [(target, source) for source, target in forward]
        low = lax.ppermute(
            lax.slice_in_dim(block, block.shape[dim] - width, None, axis=dim), axis, forward
        )
        high = lax.ppermute(lax.slice_in_dim(block, 0, width, axis=dim), axis, backward)
        block = jnp.concatenate([low, block, high], axis=dim)
    return block


def attend(block, head_windows, seg_pad, first_frame):
    count_blocks = block.shape[0]
    branches = block.shape[1]
    rows_block = block.shape[2]
    columns = block.shape[4]
    heads_here = columns // HD
    per_frame = count_blocks // F_DEV
    reach = W_MAX * per_frame
    span = 2 * W_MAX + 1
    scale = 1.0 / math.sqrt(HD)
    pairs = block[:, :, :, 1:]
    padded = padded_2(pairs, (("frame", 0),), reach)
    queries = block[:, :, :, 0].reshape(count_blocks, branches, rows_block, heads_here, HD)
    offsets = jnp.arange(span, dtype=jnp.int32) - W_MAX
    within_reach = jnp.abs(offsets)[None, None, :] <= head_windows[:, :, None]
    results = []
    for frame_number in range(F_DEV):
        query = queries[frame_number * per_frame : (frame_number + 1) * per_frame]
        window_rows = padded[frame_number * per_frame : frame_number * per_frame + span * per_frame]
        window_rows = window_rows.reshape(span * per_frame, branches, rows_block, 2, heads_here, HD)
        key_rows = window_rows[:, :, :, 0]
        value_rows = window_rows[:, :, :, 1]
        here = first_frame + frame_number
        shots = lax.dynamic_slice_in_dim(seg_pad, here, span, 0)
        own_shot = lax.dynamic_index_in_dim(seg_pad, here + W_MAX, 0, keepdims=False)
        allowed = within_reach & (shots == own_shot)[None, None, :]
        allowed = jnp.repeat(allowed, per_frame, axis=2)
        scores = (
            jnp.einsum("sbthd,ubrhd->bhstur", query, key_rows, preferred_element_type=jnp.float32)
            * scale
        )
        scores = jnp.where(allowed[:, :, None, None, :, None], scores, -1e30)
        highest = jnp.max(scores, axis=(4, 5), keepdims=True)
        expd = jnp.exp(scores - highest)
        totals = jnp.sum(expd, axis=(4, 5))
        weights = expd.astype(jnp.bfloat16)
        mixed = jnp.einsum(
            "bhstur,ubrhd->sbthd", weights, value_rows, preferred_element_type=jnp.float32
        )
        mixed = mixed / jnp.transpose(totals, (2, 0, 3, 1))[..., None]
        results.append(mixed.astype(jnp.bfloat16))
    return jnp.concatenate(results, axis=0)


def body(qkv, timestep, windows, segments):
    first_frame = lax.axis_index("frame") * F_DEV
    fill = jnp.full((W_MAX,), -1, jnp.int32)
    seg_pad = jnp.concatenate([fill, segments, fill])
    strength = 1.0 + 4.0 * timestep[0].astype(jnp.float32) / 999.0
    seq_count = lax.axis_size("seq")
    cfg_count = lax.axis_size("cfg")
    spread = lax.all_to_all(qkv, ("seq", "cfg"), split_axis=3, concat_axis=0, tiled=True)
    columns = spread.shape[3]
    heads_here = columns // HD
    block = spread.reshape(seq_count, cfg_count, spread.shape[1], 3, columns)
    start_head = (lax.axis_index("seq") * cfg_count + lax.axis_index("cfg")) * heads_here
    head_windows = lax.dynamic_slice_in_dim(windows, start_head, heads_here, 0).reshape(
        1, heads_here
    )
    attended = attend(block, head_windows, seg_pad, first_frame)
    cond = attended[:, 0].astype(jnp.float32)
    uncond = attended[:, 1].astype(jnp.float32)
    guided = (uncond + strength * (cond - uncond)).astype(jnp.bfloat16)
    own_rows = lax.all_to_all(guided, "seq", split_axis=0, concat_axis=3, tiled=True)
    return own_rows[0]


def solution(mesh):
    return jax.shard_map(
        body,
        mesh=mesh,
        in_specs=(P("cfg", ("groups", "frame", "seq"), None, None), P("groups"), P(), P("groups")),
        out_specs=P(("groups", "frame", "seq"), "cfg", None),
        check_vma=False,
    )
```

profile of v0, /device:TPU:1, one launch (start us, length us, event | category | flops | bytes accessed | tf_op | source)
XLA Modules:
  0.0 340.8 jit_solution(6959180274236141472)
XLA Ops:
  0.0 13.1 %copy.21 = bf16[1,256,3,4096]{1,2,0,3:T(4,128)(2,1)} copy(bf16[1,256,3,4096]{3,1,2,0:T(8,128)(2,1)} %param.4) | data formatting | bytes 12582912 | tf_op args[0]
  13.1 96.8 %all_to_all.30 = bf16[1,256,3,4096]{1,2,0,3:T(4,128)(2,1)S(1)} all-to-all(bf16[1,256,3,4096]{1,2,0,3:T(4,128)(2,1)} %copy.21), channel_id=1, replica_groups=mesh['groups'=2,'seq'=2,'frame'=4,'cfg'=2] {'seq','cfg'}, dimensions={3} | all-to-all | bytes 12582912 | tf_op jit(solution)/shard_map/all_to_all | solution.py:77
  110.0 0.0 copy-start.1
  110.0 0.0 copy-start.2
  110.0 3.7 %copy.22 = bf16[1,256,3,4,1024]{1,4,2,3,0:T(8,128)(2,1)} copy(bf16[1,256,3,4,1024]{1,2,4,3,0:T(4,128)(2,1)S(1)} %bitcast.109) | data formatting | bytes 12582912 | tf_op jit(solution)/shard_map/all_to_all | solution.py:77
  113.7 4.5 %slice.49 = bf16[2,2,256,2,1024]{2,4,3,1,0:T(8,128)(2,1)} slice(bf16[2,2,256,3,1024]{2,4,3,1,0:T(8,128)(2,1)} %bitcast.110), slice={[0:2], [0:2], [0:256], [1:3], [0:1024]} | slice | bytes 8388608 | tf_op jit(solution)/shard_map/slice | solution.py:36
  118.1 1.3 collective-permute-start.1
  119.4 6.6 %collective-permute-start = (bf16[2,2,256,2,1024]{2,4,3,1,0:T(8,128)(2,1)}, bf16[2,2,256,2,1024]{2,4,3,1,0:T(8,128)(2,1)}, u32[]{:S(2)}, u32[]{:S(2)}) collective-permute-start(bf16[2,2,256,2,1024]{2,4,3,1,0:T(8,128)(2,1)} %slice.49), channel_id=1, source_target_pairs={{0,2},{2,4},{4,6},{1,3},{3,5},{5,7},{8,10},{10,12},{12,14},{9,11},... | collective-permute-start | bytes 12582920 | tf_op jit(solution)/shard_map/ppermute | solution.py:18
  126.7 0.0 copy-done.1
  126.7 0.1 dynamic_slice.16
  126.8 0.0 copy-done.2
  126.8 0.1 pad_add_fusion
  126.8 0.6 fusion.35
  127.4 1.3 dynamic-slice_compare_fusion
  128.8 0.1 compare_and_fusion
  128.9 1.7 fusion.34
  130.6 81.8 %collective-permute-done.1 = bf16[2,2,256,2,1024]{2,4,3,1,0:T(8,128)(2,1)} collective-permute-done((bf16[2,2,256,2,1024]{2,4,3,1,0:T(8,128)(2,1)}, bf16[2,2,256,2,1024]{2,4,3,1,0:T(8,128)(2,1)}, u32[]{:S(2)}, u32[]{:S(2)}) %collective-permute-start.1) | collective-permute-done | bytes 4194336 | tf_op jit(solution)/shard_map/ppermute | solution.py:21
  212.3 0.9 collective-permute-done
  213.2 6.3 %pad_maximum_fusion = bf16[6,2,256,2,1024]{2,4,3,1,0:T(8,128)(2,1)S(1)} fusion(bf16[2,2,256,2,1024]{2,4,3,1,0:T(8,128)(2,1)} %collective-permute-done.1, bf16[2,2,256,2,1024]{2,4,3,1,0:T(8,128)(2,1)} %slice.49, bf16[2,2,256,2,1024]{2,4,3,1,0:T(8,128)(2,1)} %collective-permute-done), kind=kLoop, calls=%fused_computation.12 | loop fusion | flops 12582912 | bytes 25165824 | tf_op jit(solution)/shard_map/concatenate | solution.py:22
  219.5 7.4 %fusion.31 = (bf16[5,2,256,2,1024]{2,4,3,1,0:T(8,128)(2,1)}, bf16[5,2,256,2,1024]{2,4,3,1,0:T(8,128)(2,1)}) fusion(bf16[6,2,256,2,1024]{2,4,3,1,0:T(8,128)(2,1)S(1)} %pad_maximum_fusion), kind=kLoop, calls=%fused_computation.47 | loop fusion | bytes 41943040 | tf_op jit(solution)/shard_map/slice | solution.py:44
  226.9 9.7 %fusion.33 = (bf16[5,2,256,1,8,128]{2,5,4,3,1,0:T(8,128)(2,1)}, bf16[5,2,256,1,8,128]{2,5,4,3,1,0:T(8,128)(2,1)}) fusion(bf16[5,2,256,2,8,128]{2,5,4,3,1,0:T(8,128)(2,1)} %bitcast.108), kind=kLoop, calls=%fused_computation.49 | loop fusion | bytes 20971520 | tf_op jit(solution)/shard_map/slice | solution.py:47
  236.6 8.0 %copy.44 = bf16[5,2,256,1,8,128]{5,2,0,4,1,3:T(8,128)(2,1)} copy(bf16[5,2,256,1,8,128]{2,5,4,3,1,0:T(8,128)(2,1)} %get-tuple-element.10) | data formatting | bytes 10485760
  244.5 9.6 %fusion.32 = (bf16[5,2,256,1,8,128]{2,5,4,3,1,0:T(8,128)(2,1)}, bf16[5,2,256,1,8,128]{2,5,4,3,1,0:T(8,128)(2,1)}) fusion(bf16[5,2,256,2,8,128]{2,5,4,3,1,0:T(8,128)(2,1)} %bitcast.107), kind=kLoop, calls=%fused_computation.48 | loop fusion | bytes 20971520 | tf_op jit(solution)/shard_map/slice | solution.py:47
  254.2 7.9 %copy.46 = bf16[5,2,256,1,8,128]{5,2,0,4,1,3:T(8,128)(2,1)} copy(bf16[5,2,256,1,8,128]{2,5,4,3,1,0:T(8,128)(2,1)} %get-tuple-element.8) | data formatting | bytes 10485760
  262.0 12.4 %bitcast_reduce_fusion.1 = (f32[2,8,256]{2,1,0:T(8,128)S(1)}, f32[2,8,5,256,256]{4,3,2,1,0:T(8,128)}) fusion(pred[8,5]{1,0:T(8,128)(4,1)S(1)} %get-tuple-element.14, bf16[2,256,8,128,1]{1,3,4,2,0:T(8,128)(2,1)S(1)} %bitcast.113, bf16[5,2,256,1,8,128]{5,2,0,4,1,3:T(8,128)(2,1)} %copy.44), kind=kOutput, calls=%fused_computation.4 | convolution fusion | flops 1357901824 | bytes 27279400 | tf_op jit(solution)/shard_map/sbthd,ubrhd->bhstur/dot_general | solution.py:54
  274.4 4.8 %bitcast_reduce_fusion = (f32[2,8,256]{2,1,0:T(8,128)S(1)}, f32[2,8,5,256,256]{4,3,2,1,0:T(8,128)S(1)}) fusion(pred[8,5]{1,0:T(8,128)(4,1)S(1)} %get-tuple-element.13, bf16[2,256,8,128,1]{1,3,4,2,0:T(8,128)(2,1)S(1)} %bitcast.112, bf16[5,2,256,1,8,128]{5,2,0,4,1,3:T(8,128)(2,1)} %copy.46), kind=kOutput, calls=%fused_computation.1 | convolution fusion | flops 1357901824 | bytes 27279400 | tf_op jit(solution)/shard_map/sbthd,ubrhd->bhstur/dot_general | solution.py:54
  279.3 0.0 copy-start
  279.3 18.6 %fusion.2 = (f32[2,8,256]{2,1,0:T(8,128)S(1)}, f32[2,8,256]{2,1,0:T(8,128)S(1)}) fusion(f32[2,8,5,256,256]{4,3,2,1,0:T(8,128)} %get-tuple-element.20, f32[2,8,256]{2,1,0:T(8,128)S(1)} %get-tuple-element.19, pred[8,5]{1,0:T(8,128)(4,1)S(1)} %get-tuple-element.14, f32[2,8,256]{2,1,0:T(8,128)S(1)} %get-tuple-element.21, ...), kind=kLoop, calls=%fused_computation.8 | loop fusion | flops 41934848 | bytes 42008656 | tf_op jit(solution)/shard_map/reduce_sum | solution.py:60
  297.9 0.0 copy-done
  297.9 13.2 %fusion.19 = bf16[1,2,256,8,128]{2,4,3,1,0:T(8,128)(2,1)S(1)} fusion(f32[2,8,5,256,256]{4,3,2,1,0:T(8,128)} %get-tuple-element.20, f32[2,8,256]{2,1,0:T(8,128)S(1)} %get-tuple-element.19, pred[8,5]{1,0:T(8,128)(4,1)S(1)} %get-tuple-element.14, bf16[5,2,256,1,8,128]{2,5,4,3,1,0:T(8,128)(2,1)} %get-tuple-element.9, f32[2,256,8]{1,2,0:T(8,128)S(1)} %bitcast.116), kind=kOutput, calls=%fused_computation.32 | convolution fusion | flops 1364197376 | bytes 27295784 | tf_op jit(solution)/shard_map/bhstur,ubrhd->sbthd/dot_general | solution.py:62
  311.2 13.2 %fusion.18 = bf16[1,2,256,8,128]{2,4,3,1,0:T(8,128)(2,1)S(1)} fusion(f32[2,8,5,256,256]{4,3,2,1,0:T(8,128)} %copy-done, f32[2,8,256]{2,1,0:T(8,128)S(1)} %get-tuple-element.21, pred[8,5]{1,0:T(8,128)(4,1)S(1)} %get-tuple-element.13, bf16[5,2,256,1,8,128]{2,5,4,3,1,0:T(8,128)(2,1)} %get-tuple-element.7, f32[2,256,8]{1,2,0:T(8,128)S(1)} %bitcast.115), kind=kOutput, calls=%fused_computation.30 | convolution fusion | flops 1364197376 | bytes 27295784 | tf_op jit(solution)/shard_map/bhstur,ubrhd->sbthd/dot_general | solution.py:62
  324.4 0.4 fusion.17
  324.8 14.2 %all_to_all.31 = bf16[2,256,8,128]{1,3,2,0:T(8,128)(2,1)S(1)} all-to-all(bf16[2,256,8,128]{1,3,2,0:T(8,128)(2,1)S(1)} %fusion.17), channel_id=1, replica_groups=mesh['groups'=2,'seq'=2,'frame'=4,'cfg'=2] {'seq'}, dimensions={0} | all-to-all | bytes 2097152 | tf_op jit(solution)/shard_map/all_to_all | solution.py:89
  339.1 1.8 copy.32
  (2 shorter events, 0.0 us)
Async XLA Ops:
  110.0 16.7 %copy-start.1 = (s32[32]{0:T(128)S(1)}, s32[32]{0:T(128)}, u32[]{:S(2)}) copy-start(s32[32]{0:T(128)} %param.6) | copy-start | bytes 388
  110.0 16.8 %copy-start.2 = (s32[8]{0:T(128)S(1)}, s32[8]{0:T(128)}, u32[]{:S(2)}) copy-start(s32[8]{0:T(128)} %param.7) | copy-start | bytes 100
  118.1 94.2 %collective-permute-start.1 = (bf16[2,2,256,2,1024]{2,4,3,1,0:T(8,128)(2,1)}, bf16[2,2,256,2,1024]{2,4,3,1,0:T(8,128)(2,1)}, u32[]{:S(2)}, u32[]{:S(2)}) collective-permute-start(bf16[2,2,256,2,1024]{2,4,3,1,0:T(8,128)(2,1)} %slice.49), channel_id=1, source_target_pairs={{2,0},{4,2},{6,4},{3,1},{5,3},{7,5},{10,8},{12,10},{14,12},{11,9},... | collective-permute-start | bytes 12582920 | tf_op jit(solution)/shard_map/ppermute | solution.py:21
  119.4 93.8 %collective-permute-start = (bf16[2,2,256,2,1024]{2,4,3,1,0:T(8,128)(2,1)}, bf16[2,2,256,2,1024]{2,4,3,1,0:T(8,128)(2,1)}, u32[]{:S(2)}, u32[]{:S(2)}) collective-permute-start(bf16[2,2,256,2,1024]{2,4,3,1,0:T(8,128)(2,1)} %slice.49), channel_id=1, source_target_pairs={{0,2},{2,4},{4,6},{1,3},{3,5},{5,7},{8,10},{10,12},{12,14},{9,11},... | collective-permute-start | bytes 12582920 | tf_op jit(solution)/shard_map/ppermute | solution.py:18
  279.3 18.6 %copy-start = (f32[2,8,5,256,256]{4,3,2,1,0:T(8,128)}, f32[2,8,5,256,256]{4,3,2,1,0:T(8,128)S(1)}, u32[]{:S(2)}) copy-start(f32[2,8,5,256,256]{4,3,2,1,0:T(8,128)S(1)} %get-tuple-element.22) | copy-start | bytes 62914564
where the time goes:
time: 346 us; the launch traced here: 341 us
  blocking collectives  111 us (32%)
  waiting for transfers between devices  82.7 us (24%)
  local copies, waits for them, and re-layouts  68 us (20%)
  matrix products  43.7 us (13%)
  other arithmetic  26.8 us (8%)
  starting transfers between devices  7.88 us (2%)
    all_to_all x1, blocking collectives, body(): lax.all_to_all(qkv, ('seq', 'cfg'), split_axis=3, concat_axis=0, tiled=True)  96.8 us
    ppermute x1, waiting for transfers between devices, padded_2(): lax.ppermute(lax.slice_in_dim(block, 0, width, axis=dim), axis, backward)  81.8 us
    unnamed x9, local copies, waits for them, and re-layouts  29 us
    dot_general x2, matrix products, attend(): jnp.einsum('bhstur,ubrhd->sbthd', weights, value_rows, preferred_element_...  26.5 us
    slice x2, local copies, waits for them, and re-layouts, attend(): value_rows = window_rows[:, :, :, 1]  19.3 us
    reduce_sum x1, other arithmetic, attend(): totals = jnp.sum(expd, axis=(4, 5))  18.6 us
    dot_general x2, matrix products, attend(): jnp.einsum('sbthd,ubrhd->bhstur', query, key_rows, preferred_element_type...  17.2 us
    all_to_all x1, blocking collectives, body(): lax.all_to_all(guided, 'seq', split_axis=0, concat_axis=3, tiled=True)  14.2 us
  transfers between devices with their start and end apart: 2, of which 2 were waited for; matrix products, arithmetic and copies ran while one was open for 1% of the time, Pallas kernels for 0%

commit v1 on v0

v1 whole, which is shorter than its diff:
```python
import functools
import math

import jax
import jax.numpy as jnp
from jax import lax
from jax.experimental import pallas as pl
from jax.experimental.pallas import tpu as pltpu
from jax.sharding import PartitionSpec as P

HD = 128
W_MAX = 2
NEG = -1e30
LOG2E = 1.4426950408889634
MESH = pl.DeviceIdType.MESH


def kernel(
    dims, x_ref, time_ref, win_ref, seg_ref, out_ref,
    kv, qb, gb, kv_sem, q_sem, halo_sem, out_sem, a2a_send, own_send, relay_send, out_send,
):
    S, C, F, heads, tl, frames_here = dims
    rows = S * tl
    per_frame = rows // frames_here
    span = (2 * W_MAX + 1) * per_frame
    frames = F * frames_here
    s = lax.axis_index("seq")
    c = lax.axis_index("cfg")
    f = lax.axis_index("frame")
    partners = [(ds, dc) for ds in range(S) for dc in range(C) if ds or dc]
    others = [(i, ds, dc) for i, (ds, dc) in enumerate(partners) if ds]

    def at(ds, dc):
        return lax.rem(s + ds, S), lax.rem(c + dc, C)

    def columns(group, h):
        return pl.ds(pl.multiple_of((group * heads + h) * HD, HD), HD)

    def token_rows(base, piece):
        return pl.ds(pl.multiple_of(base + piece * tl, tl), tl)

    barrier = pltpu.get_barrier_semaphore()
    for ds, dc in partners:
        s2, c2 = at(ds, dc)
        pl.semaphore_signal(
            barrier, inc=1, device_id={"seq": s2, "cfg": c2}, device_id_type=MESH
        )
    for step in (-1, 1):
        @pl.when((f + step >= 0) & (f + step < F))
        def _():
            for dc in range(C):
                pl.semaphore_signal(
                    barrier, inc=1,
                    device_id={"frame": f + step, "cfg": lax.rem(c + dc, C)},
                    device_id_type=MESH,
                )
    beside = jnp.where(f > 0, C, 0) + jnp.where(f < F - 1, C, 0)
    pl.semaphore_wait(barrier, len(partners) + beside)

    def send_kv(i, ds, dc, h):
        s2, c2 = at(ds, dc)
        return pltpu.make_async_remote_copy(
            src_ref=x_ref.at[pl.ds(1, 2), :, columns(s2 * C + c2, h)],
            dst_ref=kv.at[h, c, :, token_rows(rows, s), :],
            send_sem=a2a_send.at[0, h, i],
            recv_sem=kv_sem.at[h, s, c],
            device_id={"seq": s2, "cfg": c2}, device_id_type=MESH,
        )

    def send_q(i, ds, dc, h):
        s2, c2 = at(ds, dc)
        return pltpu.make_async_remote_copy(
            src_ref=x_ref.at[0, :, columns(s2 * C + c2, h)],
            dst_ref=qb.at[h, c, token_rows(0, s), :],
            send_sem=a2a_send.at[1, h, i],
            recv_sem=q_sem.at[h, s, c],
            device_id={"seq": s2, "cfg": c2}, device_id_type=MESH,
        )

    def own_kv(h):
        return pltpu.make_async_copy(
            x_ref.at[pl.ds(1, 2), :, columns(s * C + c, h)],
            kv.at[h, c, :, token_rows(rows, s), :],
            kv_sem.at[h, s, c],
        )

    def own_q(h):
        return pltpu.make_async_copy(
            x_ref.at[0, :, columns(s * C + c, h)],
            qb.at[h, c, token_rows(0, s), :],
            q_sem.at[h, s, c],
        )

    def halo_base(side):
        return 0 if side == 0 else 2 * rows

    def send_halo(side, dc, h):
        c2 = lax.rem(c + dc, C)
        return pltpu.make_async_remote_copy(
            src_ref=x_ref.at[pl.ds(1, 2), :, columns(s * C + c2, h)],
            dst_ref=kv.at[h, c, :, token_rows(halo_base(side), s), :],
            send_sem=own_send.at[side, h, dc],
            recv_sem=halo_sem.at[side, h, s, c],
            device_id={"frame": f + (1 if side == 0 else -1), "cfg": c2}, device_id_type=MESH,
        )

    def relay(side, i, ds, dc, h):
        s2, b = at(ds, dc)
        return pltpu.make_async_remote_copy(
            src_ref=kv.at[h, b, :, token_rows(rows, s2), :],
            dst_ref=kv.at[h, b, :, token_rows(halo_base(side), s2), :],
            send_sem=relay_send.at[side, h, i],
            recv_sem=halo_sem.at[side, h, s2, b],
            device_id={"frame": f + (1 if side == 0 else -1)}, device_id_type=MESH,
        )

    def send_out(ds, h):
        s2 = lax.rem(s + ds, S)
        return pltpu.make_async_remote_copy(
            src_ref=gb.at[h, token_rows(0, s2), :],
            dst_ref=out_ref.at[h, :, pl.ds(pl.multiple_of(s * HD, HD), HD)],
            send_sem=out_send.at[h, ds - 1],
            recv_sem=out_sem.at[h, s],
            device_id={"seq": s2}, device_id_type=MESH,
        )

    def recv(ref, sem):
        pltpu.make_async_remote_copy(
            src_ref=ref, dst_ref=ref, send_sem=sem, recv_sem=sem,
            device_id={"seq": s}, device_id_type=MESH,
        ).wait_recv()

    up_ok = f < F - 1
    down_ok = f > 0

    @pl.loop(0, heads)
    def _(h):
        for i, (ds, dc) in enumerate(partners):
            send_kv(i, ds, dc, h).start()
        for side, ok in ((0, up_ok), (1, down_ok)):
            @pl.when(ok)
            def _():
                for dc in range(C):
                    send_halo(side, dc, h).start()
        own_kv(h).start()

    @pl.loop(0, heads)
    def _(h):
        for i, (ds, dc) in enumerate(partners):
            send_q(i, ds, dc, h).start()
        own_q(h).start()

    for edge, base in ((f == 0, 0), (f == F - 1, 2 * rows)):
        @pl.when(edge)
        def _():
            @pl.loop(0, heads)
            def _(h):
                kv[h, :, :, pl.ds(base, rows), :] = jnp.zeros((C, 2, rows, HD), kv.dtype)

    @pl.loop(0, heads)
    def _(h):
        for i, ds, dc in others:
            s2, b = at(ds, dc)
            recv(kv.at[h, b, :, token_rows(rows, s2), :], kv_sem.at[h, s2, b])
            for side, ok in ((0, up_ok), (1, down_ok)):
                @pl.when(ok)
                def _():
                    relay(side, i, ds, dc, h).start()

    now = jnp.full((1, HD), time_ref[0], jnp.int32).astype(jnp.float32)
    strength = 1.0 + 4.0 * now / 999.0
    factor = LOG2E / math.sqrt(HD)

    @pl.loop(0, heads)
    def _(h):
        own_kv(h).wait()
        own_q(h).wait()
        for ds, dc in partners:
            s2, b = at(ds, dc)
            if not ds:
                recv(kv.at[h, b, :, token_rows(rows, s2), :], kv_sem.at[h, s2, b])
            recv(qb.at[h, b, token_rows(0, s2), :], q_sem.at[h, s2, b])
        for side, ok in ((0, down_ok), (1, up_ok)):
            @pl.when(ok)
            def _():
                for ds in range(S):
                    for dc in range(C):
                        s2, b = at(ds, dc)
                        recv(
                            kv.at[h, b, :, token_rows(halo_base(side), s2), :],
                            halo_sem.at[side, h, s2, b],
                        )
        window = win_ref[(s * C + c) * heads + h]
        for number in range(frames_here):
            here = f * frames_here + number
            own_shot = seg_ref[here]
            pieces = []
            for offset in range(-W_MAX, W_MAX + 1):
                there = here + offset
                shot = seg_ref[jnp.clip(there, 0, frames - 1)]
                allowed = (
                    (there >= 0) & (there < frames) & (shot == own_shot) & (abs(offset) <= window)
                )
                pieces.append(jnp.full((1, per_frame), jnp.where(allowed, 0.0, NEG), jnp.float32))
            bias = jnp.concatenate(pieces, axis=1)
            start = (frames_here + number - W_MAX) * per_frame
            mixed = []
            for b in range(C):
                query = qb[h, b, pl.ds(number * per_frame, per_frame), :]
                keys = kv[h, b, 0, pl.ds(start, span), :]
                values = kv[h, b, 1, pl.ds(start, span), :]
                scores = lax.dot_general(
                    query, keys, (((1,), (1,)), ((), ())), preferred_element_type=jnp.float32
                ) + bias
                top = jnp.max(scores, axis=1, keepdims=True)
                expd = jnp.exp2((scores - top) * factor)
                total = jnp.sum(expd, axis=1, keepdims=True)
                part = jnp.dot(
                    expd.astype(jnp.bfloat16), values, preferred_element_type=jnp.float32
                )
                mixed.append((part / total).astype(jnp.bfloat16).astype(jnp.float32))
            cond, uncond = mixed
            gb[h, pl.ds(number * per_frame, per_frame), :] = (
                uncond + strength * (cond - uncond)
            ).astype(jnp.bfloat16)
        for ds in range(1, S):
            send_out(ds, h).start()
        out_ref[h, :, pl.ds(pl.multiple_of(s * HD, HD), HD)] = gb[h, token_rows(0, s), :]

    @pl.loop(0, heads)
    def _(h):
        for i, (ds, dc) in enumerate(partners):
            send_kv(i, ds, dc, h).wait_send()
            send_q(i, ds, dc, h).wait_send()
        for side, ok in ((0, up_ok), (1, down_ok)):
            @pl.when(ok)
            def _():
                for dc in range(C):
                    send_halo(side, dc, h).wait_send()
                for i, ds, dc in others:
                    relay(side, i, ds, dc, h).wait_send()
        for ds in range(1, S):
            s2 = lax.rem(s + ds, S)
            send_out(ds, h).wait_send()
            recv(out_ref.at[h, :, pl.ds(pl.multiple_of(s2 * HD, HD), HD)], out_sem.at[h, s2])


def body(qkv, timestep, windows, segments):
    S, C, F = (lax.axis_size(axis) for axis in ("seq", "cfg", "frame"))
    x = jnp.transpose(qkv[0], (1, 0, 2))
    tl = x.shape[1]
    heads = x.shape[2] // HD // (S * C)
    frames_here = segments.shape[0] // F
    assert frames_here >= W_MAX and frames_here == W_MAX
    rows = S * tl
    n = S * C - 1
    dma = pltpu.SemaphoreType.DMA
    out = pl.pallas_call(
        functools.partial(kernel, (S, C, F, heads, tl, frames_here)),
        out_shape=jax.ShapeDtypeStruct((heads, tl, S * HD), jnp.bfloat16),
        in_specs=[pl.BlockSpec(memory_space=pl.ANY)]
        + [pl.BlockSpec(memory_space=pltpu.SMEM)] * 3,
        out_specs=pl.BlockSpec(memory_space=pltpu.VMEM),
        scratch_shapes=[
            pltpu.VMEM((heads, C, 2, 3 * rows, HD), jnp.bfloat16),
            pltpu.VMEM((heads, C, rows, HD), jnp.bfloat16),
            pltpu.VMEM((heads, rows, HD), jnp.bfloat16),
            dma((heads, S, C)),
            dma((heads, S, C)),
            dma((2, heads, S, C)),
            dma((heads, S)),
            dma((2, heads, n)),
            dma((2, heads, C)),
            dma((2, heads, n)),
            dma((heads, max(S - 1, 1))),
        ],
        compiler_params=pltpu.CompilerParams(
            collective_id=0, has_side_effects=True, vmem_limit_bytes=48 * 2**20
        ),
        name="guided_attention",
    )(x, timestep, windows, segments)
    return jnp.transpose(out, (1, 0, 2))


def solution(mesh):
    return jax.shard_map(
        body,
        mesh=mesh,
        in_specs=(P("cfg", ("groups", "frame", "seq"), None, None), P("groups"), P(), P("groups")),
        out_specs=P(("groups", "frame", "seq"), "cfg", None),
        check_vma=False,
    )
```

time: 346 us -> 109 us (0.32)
  blocking collectives: 111 us -> 0 us
  Pallas kernels: 0 us -> 103 us
  waiting for transfers between devices: 82.7 us -> 0 us
  local copies, waits for them, and re-layouts: 68 us -> 2.86 us
  matrix products: 43.7 us -> 0 us
  other arithmetic: 26.8 us -> 0 us
  starting transfers between devices: 7.88 us -> 0 us
    all_to_all x2 -> x0, blocking collectives: 111 us -> none  [the longest x1 96.8 us: body(): lax.all_to_all(qkv, ('seq', 'cfg'), split_axis=3, concat_axis=0, tiled=True)]
    pallas_call x0 -> x1, Pallas kernels: none -> 103 us  [body(): pl.pallas_call(functools.partial(kernel, (S, C, F, heads, tl, frames_here...]
    ppermute x2 -> x0, waiting for transfers between devices: 82.7 us -> none  [the longest x1 81.8 us: padded_2(): lax.ppermute(lax.slice_in_dim(block, 0, width, axis=dim), axis, backward)]
    dot_general x4 -> x0, matrix products: 43.7 us -> none  [the longest x2 26.5 us: attend(): jnp.einsum('bhstur,ubrhd->sbthd', weights, value_rows, preferred_element_...]
    slice x5 -> x0, local copies, waits for them, and re-layouts: 32.8 us -> none  [the longest x2 19.3 us: attend(): value_rows = window_rows[:, :, :, 1]]
    unnamed x9 -> x4, local copies, waits for them, and re-layouts: 29 us -> 1.3 us
    reduce_sum x1 -> x0, other arithmetic: 18.6 us -> none  [attend(): totals = jnp.sum(expd, axis=(4, 5))]
    ppermute x2 -> x0, starting transfers between devices: 7.88 us -> none  [the longest x1 6.6 us: padded_2(): lax.ppermute(lax.slice_in_dim(block, block.shape[dim] - width, None, axis...]
  transfers between devices with their start and end apart: 2 -> 0, of which waited for: 2 -> 0; matrix products, arithmetic and copies ran while one was open for 1% -> 0% of each run, Pallas kernels for 0% -> 0%
where the time goes in v1:
time: 109 us; the launch traced here: 107 us
  Pallas kernels  103 us (94%)
  local copies, waits for them, and re-layouts  2.86 us (3%)
    pallas_call x1, Pallas kernels, body(): pl.pallas_call(functools.partial(kernel, (S, C, F, heads, tl, frames_here...  103 us

profile of v1, /device:TPU:1, one launch (start us, length us, event | category | flops | bytes accessed | tf_op | source)
XLA Modules:
  0.0 106.8 jit_solution(900624097357462269)
XLA Ops:
  0.7 0.0 copy-start
  0.7 0.6 copy-done
  1.3 0.0 copy-start.1
  1.3 0.7 copy-done.1
  2.0 103.3 %guided_attention.1 = bf16[8,256,256]{2,1,0:T(8,128)(2,1)S(1)} custom-call(bf16[3,256,4096]{2,1,0:T(8,128)(2,1)} %bitcast.5, s32[1]{0:T(128)S(6)} %copy.6.time_ref, s32[32]{0:T(128)S(1)} %copy-done, s32[8]{0:T(128)S(1)} %copy-done.1), custom_call_target="tpu_custom_call" | custom-call | tf_op jit(solution)/shard_map/guided_attention/pallas_call | solution.py:258
  105.3 1.6 %copy.5 = bf16[256,8,256]{2,1,0:T(8,128)(2,1)} copy(bf16[256,8,256]{2,0,1:T(8,128)(2,1)S(1)} %bitcast.4) | data formatting | bytes 2097152 | tf_op jit(solution)/shard_map/transpose | solution.py:282
Async XLA Ops:
  0.7 0.7 copy-start
  1.3 0.7 copy-start.1

commit v2 on v1

v2 whole, which is shorter than its diff:
```python
import functools
import math

import jax
import jax.numpy as jnp
from jax import lax
from jax.experimental import pallas as pl
from jax.experimental.pallas import tpu as pltpu
from jax.sharding import PartitionSpec as P

HD = 128
W_MAX = 2
NEG = -1e30
LOG2E = 1.4426950408889634
MESH = pl.DeviceIdType.MESH


def gather_kernel(heads_all, levels, x_ref, win_ref, out_ref, sem):
    def copy(head, slot):
        return pltpu.make_async_copy(
            x_ref.at[:, :, pl.ds(pl.multiple_of(head * HD, HD), HD)], out_ref.at[slot], sem
        )

    def place(level):
        def step(head, slot):
            hit = win_ref[head] == level

            @pl.when(hit)
            def _():
                copy(head, slot).start()

            return slot + hit.astype(jnp.int32)

        return step

    slot = jnp.int32(0)
    for level in range(levels, -1, -1):
        slot = lax.fori_loop(0, heads_all, place(level), slot)
    pltpu.make_async_copy(out_ref, out_ref, sem).wait()


def kernel(
    dims, x_ref, time_ref, win_ref, seg_ref, out_ref,
    kv, qb, gb, lb, every, rank_ref,
    kv_sem, q_sem, halo_sem, out_sem, a2a_send, own_send, relay_send, out_send, core_send,
    l_sem, l_send,
):
    S, C, F, heads, tl, frames_here, wide, near = dims
    groups = S * C
    rows = S * tl
    per_frame = rows // frames_here
    frames = F * frames_here
    s = lax.axis_index("seq")
    c = lax.axis_index("cfg")
    f = lax.axis_index("frame")
    partners = [(ds, dc) for ds in range(S) for dc in range(C) if ds or dc]
    others = [(i, ds, dc) for i, (ds, dc) in enumerate(partners) if ds]
    up_ok = f < F - 1
    down_ok = f > 0

    def at(ds, dc):
        return lax.rem(s + ds, S), lax.rem(c + dc, C)

    def rank(h, s2, c2):
        return h * groups + s2 * C + c2

    def token_rows(base, piece):
        return pl.ds(pl.multiple_of(base + piece * tl, tl), tl)

    barrier = pltpu.get_barrier_semaphore()
    for ds, dc in partners:
        s2, c2 = at(ds, dc)
        pl.semaphore_signal(
            barrier, inc=1, device_id={"seq": s2, "cfg": c2}, device_id_type=MESH
        )
    for step in (-1, 1):
        @pl.when((f + step >= 0) & (f + step < F))
        def _():
            for dc in range(C):
                pl.semaphore_signal(
                    barrier, inc=1,
                    device_id={"frame": f + step, "cfg": lax.rem(c + dc, C)},
                    device_id_type=MESH,
                )
    beside = jnp.where(f > 0, C, 0) + jnp.where(f < F - 1, C, 0)
    pl.semaphore_wait(barrier, len(partners) + beside)

    def send_kv(i, ds, dc, h):
        s2, c2 = at(ds, dc)
        return pltpu.make_async_remote_copy(
            src_ref=x_ref.at[rank(h, s2, c2), pl.ds(1, 2)],
            dst_ref=kv.at[h, c, :, token_rows(rows, s), :],
            send_sem=a2a_send.at[0, h, i],
            recv_sem=kv_sem.at[h, s, c],
            device_id={"seq": s2, "cfg": c2}, device_id_type=MESH,
        )

    def send_q(i, ds, dc, h):
        s2, c2 = at(ds, dc)
        return pltpu.make_async_remote_copy(
            src_ref=x_ref.at[rank(h, s2, c2), 0],
            dst_ref=qb.at[h, c, token_rows(0, s), :],
            send_sem=a2a_send.at[1, h, i],
            recv_sem=q_sem.at[h, s, c],
            device_id={"seq": s2, "cfg": c2}, device_id_type=MESH,
        )

    def own_kv(h):
        return pltpu.make_async_copy(
            x_ref.at[rank(h, s, c), pl.ds(1, 2)],
            kv.at[h, c, :, token_rows(rows, s), :],
            kv_sem.at[h, s, c],
        )

    def own_q(h):
        return pltpu.make_async_copy(
            x_ref.at[rank(h, s, c), 0], qb.at[h, c, token_rows(0, s), :], q_sem.at[h, s, c]
        )

    def halo_base(side):
        return 0 if side == 0 else 2 * rows

    def neighbour(side):
        return f + (1 if side == 0 else -1)

    def send_halo(side, dc, h):
        c2 = lax.rem(c + dc, C)
        return pltpu.make_async_remote_copy(
            src_ref=x_ref.at[rank(h, s, c2), pl.ds(1, 2)],
            dst_ref=kv.at[h, c, :, token_rows(halo_base(side), s), :],
            send_sem=own_send.at[side, h, dc],
            recv_sem=halo_sem.at[side, h, s, c],
            device_id={"frame": neighbour(side), "cfg": c2}, device_id_type=MESH,
        )

    def relay(side, i, ds, dc, h):
        s2, b = at(ds, dc)
        return pltpu.make_async_remote_copy(
            src_ref=kv.at[h, b, :, token_rows(rows, s2), :],
            dst_ref=kv.at[h, b, :, token_rows(halo_base(side), s2), :],
            send_sem=relay_send.at[side, h, i],
            recv_sem=halo_sem.at[side, h, s2, b],
            device_id={"frame": neighbour(side)}, device_id_type=MESH,
        )

    def crosses(side, s2, reach):
        if reach == W_MAX:
            return s2 >= 0
        return s2 == (S - 1 if side == 0 else 0)

    def send_out(ds, h):
        s2 = lax.rem(s + ds, S)
        return pltpu.make_async_remote_copy(
            src_ref=gb.at[h, token_rows(0, s2), :],
            dst_ref=every.at[rank(h, s, c)],
            send_sem=out_send.at[h, ds - 1],
            recv_sem=out_sem.at[rank(h, s, c)],
            device_id={"seq": s2}, device_id_type=MESH,
        )

    def send_core(h, s2, dc, src):
        return pltpu.make_async_remote_copy(
            src_ref=src,
            dst_ref=every.at[rank(h, s2, c)],
            send_sem=core_send.at[h, s2, dc - 1],
            recv_sem=out_sem.at[rank(h, s2, c)],
            device_id={"cfg": lax.rem(c + dc, C)}, device_id_type=MESH,
        )

    def send_local(h, s2, dc):
        c2 = lax.rem(c + dc, C)
        return pltpu.make_async_remote_copy(
            src_ref=x_ref.at[rank(h, s2, c2)],
            dst_ref=lb.at[h - near, s2, c],
            send_sem=l_send.at[h - near, s2, dc],
            recv_sem=l_sem.at[h - near, s2, c],
            device_id={"cfg": c2}, device_id_type=MESH,
        )

    def own_local(h, s2):
        return pltpu.make_async_copy(
            x_ref.at[rank(h, s2, c)], lb.at[h - near, s2, c], l_sem.at[h - near, s2, c]
        )

    def recv(ref, sem):
        pltpu.make_async_remote_copy(
            src_ref=ref, dst_ref=ref, send_sem=sem, recv_sem=sem,
            device_id={"seq": s}, device_id_type=MESH,
        ).wait_recv()

    phases = ((0, wide, W_MAX), (wide, near, 1))
    sides = ((0, up_ok), (1, down_ok))

    for lo, hi, reach in phases:
        @pl.loop(lo, hi)
        def _(h):
            for i, (ds, dc) in enumerate(partners):
                send_kv(i, ds, dc, h).start()
            for side, ok in sides:
                @pl.when(ok & crosses(side, s, reach))
                def _():
                    for dc in range(C):
                        send_halo(side, dc, h).start()
            own_kv(h).start()

    @pl.loop(near, heads)
    def _(h):
        for s2 in range(S):
            for dc in range(1, C):
                send_local(h, s2, dc).start()
            own_local(h, s2).start()

    @pl.loop(0, near)
    def _(h):
        for i, (ds, dc) in enumerate(partners):
            send_q(i, ds, dc, h).start()
        own_q(h).start()

    for edge, base in ((f == 0, 0), (f == F - 1, 2 * rows)):
        @pl.when(edge)
        def _():
            @pl.loop(0, near)
            def _(h):
                kv[h, :, :, pl.ds(base, rows), :] = jnp.zeros((C, 2, rows, HD), kv.dtype)

    many = [jnp.int32(0)] * (W_MAX + 1)
    for head in range(heads * groups):
        for level in range(W_MAX + 1):
            many[level] = many[level] + jnp.where(win_ref[head] >= level, 1, 0)
    place = [many[level + 1] if level < W_MAX else jnp.int32(0) for level in range(W_MAX + 1)]
    for head in range(heads * groups):
        mine = place[0]
        for level in range(1, W_MAX + 1):
            mine = jnp.where(win_ref[head] == level, place[level], mine)
        rank_ref[head] = mine
        for level in range(W_MAX + 1):
            place[level] = place[level] + jnp.where(win_ref[head] == level, 1, 0)

    now = jnp.full((1, HD), time_ref[0], jnp.int32).astype(jnp.float32)
    strength = 1.0 + 4.0 * now / 999.0
    factor = LOG2E / math.sqrt(HD)

    def attend(query, keys, values, bias):
        scores = lax.dot_general(
            query, keys, (((1,), (1,)), ((), ())), preferred_element_type=jnp.float32
        )
        if bias is not None:
            scores = scores + bias
        top = jnp.max(scores, axis=1, keepdims=True)
        expd = jnp.exp2((scores - top) * factor)
        total = jnp.sum(expd, axis=1, keepdims=True)
        part = jnp.dot(expd.astype(jnp.bfloat16), values, preferred_element_type=jnp.float32)
        return (part / total).astype(jnp.bfloat16).astype(jnp.float32)

    def guide(cond, uncond):
        return (uncond + strength * (cond - uncond)).astype(jnp.bfloat16)

    @pl.loop(near, heads)
    def _(h):
        for s2 in range(S):
            own_local(h, s2).wait()
            for dc in range(1, C):
                b = lax.rem(c + dc, C)
                recv(lb.at[h - near, s2, b], l_sem.at[h - near, s2, b])
            cond, uncond = [
                attend(lb[h - near, s2, b, 0], lb[h - near, s2, b, 1], lb[h - near, s2, b, 2], None)
                for b in range(C)
            ]
            every[rank(h, s2, c)] = guide(cond, uncond)
            for dc in range(1, C):
                send_core(h, s2, dc, every.at[rank(h, s2, c)]).start()

    for lo, hi, reach in phases:
        @pl.loop(lo, hi)
        def _(h):
            for i, ds, dc in others:
                s2, b = at(ds, dc)
                recv(kv.at[h, b, :, token_rows(rows, s2), :], kv_sem.at[h, s2, b])
                for side, ok in sides:
                    @pl.when(ok & crosses(side, s2, reach))
                    def _():
                        relay(side, i, ds, dc, h).start()

    def hand_on(h):
        for ds in range(1, S):
            s2 = lax.rem(s + ds, S)
            ref = every.at[rank(h, s2, c)]
            recv(ref, out_sem.at[rank(h, s2, c)])
            for dc in range(1, C):
                send_core(h, s2, dc, ref).start()

    for lo, hi, reach in phases:
        @pl.loop(lo, hi)
        def _(h):
            own_kv(h).wait()
            own_q(h).wait()
            for ds, dc in partners:
                s2, b = at(ds, dc)
                if not ds:
                    recv(kv.at[h, b, :, token_rows(rows, s2), :], kv_sem.at[h, s2, b])
                recv(qb.at[h, b, token_rows(0, s2), :], q_sem.at[h, s2, b])
            for side, ok in ((0, down_ok), (1, up_ok)):
                for ds in range(S):
                    s2 = lax.rem(s + ds, S)

                    @pl.when(ok & crosses(side, s2, reach))
                    def _():
                        for b in range(C):
                            recv(
                                kv.at[h, b, :, token_rows(halo_base(side), s2), :],
                                halo_sem.at[side, h, s2, b],
                            )
            me = rank(h, s, c)
            window = jnp.int32(0)
            for level in range(1, W_MAX + 1):
                window = window + jnp.where(me < many[level], 1, 0)
            for number in range(frames_here):
                here = f * frames_here + number
                own_shot = seg_ref[here]
                pieces = []
                for offset in range(-reach, reach + 1):
                    there = here + offset
                    shot = seg_ref[jnp.clip(there, 0, frames - 1)]
                    allowed = (
                        (there >= 0) & (there < frames)
                        & (shot == own_shot) & (abs(offset) <= window)
                    )
                    pieces.append(
                        jnp.full((1, per_frame), jnp.where(allowed, 0.0, NEG), jnp.float32)
                    )
                bias = jnp.concatenate(pieces, axis=1)
                keys = pl.ds((frames_here + number - reach) * per_frame, len(pieces) * per_frame)
                mine = pl.ds(number * per_frame, per_frame)
                cond, uncond = [
                    attend(qb[h, b, mine, :], kv[h, b, 0, keys, :], kv[h, b, 1, keys, :], bias)
                    for b in range(C)
                ]
                gb[h, mine, :] = guide(cond, uncond)
            for ds in range(1, S):
                send_out(ds, h).start()
            for dc in range(1, C):
                send_core(h, s, dc, gb.at[h, token_rows(0, s), :]).start()
            every[me] = gb[h, token_rows(0, s), :]

            @pl.when(h > 0)
            def _():
                hand_on(h - 1)

    hand_on(near - 1)

    @pl.loop(0, heads)
    def _(h):
        for s2 in range(S):
            for dc in range(1, C):
                r = rank(h, s2, lax.rem(c + dc, C))
                recv(every.at[r], out_sem.at[r])

    half = heads
    for s2 in range(S):
        for i in range(half):
            head = s2 * (C * half) + c * half + i
            out_ref[i, :, s2 * HD : (s2 + 1) * HD] = every[rank_ref[head]]

    for lo, hi, reach in phases:
        @pl.loop(lo, hi)
        def _(h):
            for i, (ds, dc) in enumerate(partners):
                send_kv(i, ds, dc, h).wait_send()
                send_q(i, ds, dc, h).wait_send()
            for side, ok in sides:
                @pl.when(ok & crosses(side, s, reach))
                def _():
                    for dc in range(C):
                        send_halo(side, dc, h).wait_send()
                for i, ds, dc in others:
                    s2, b = at(ds, dc)

                    @pl.when(ok & crosses(side, s2, reach))
                    def _():
                        relay(side, i, ds, dc, h).wait_send()
            for ds in range(1, S):
                send_out(ds, h).wait_send()

    @pl.loop(0, heads)
    def _(h):
        for s2 in range(S):
            for dc in range(1, C):
                send_core(h, s2, dc, every.at[rank(h, s2, c)]).wait_send()

    @pl.loop(near, heads)
    def _(h):
        for s2 in range(S):
            for dc in range(1, C):
                send_local(h, s2, dc).wait_send()


def body(qkv, timestep, windows, segments):
    S, C, F = (lax.axis_size(axis) for axis in ("seq", "cfg", "frame"))
    x = jnp.transpose(qkv[0], (1, 0, 2))
    tl = x.shape[1]
    heads = x.shape[2] // HD // (S * C)
    frames_here = segments.shape[0] // F
    assert frames_here == W_MAX and heads * S * C * HD == x.shape[2]
    rows = S * tl
    groups = S * C
    n = groups - 1
    dma = pltpu.SemaphoreType.DMA
    ordered = pl.pallas_call(
        functools.partial(gather_kernel, heads * groups, W_MAX),
        out_shape=jax.ShapeDtypeStruct((heads * groups, 3, tl, HD), x.dtype),
        in_specs=[pl.BlockSpec(memory_space=pl.ANY), pl.BlockSpec(memory_space=pltpu.SMEM)],
        out_specs=pl.BlockSpec(memory_space=pltpu.VMEM),
        scratch_shapes=[dma],
        name="order_heads",
        compiler_params=pltpu.CompilerParams(vmem_limit_bytes=56 * 2**20),
    )(x, windows)

    def run(wide, near, number):
        kept = max(heads - near, 1)

        def call(ordered, timestep, windows, segments):
            return pl.pallas_call(
                functools.partial(kernel, (S, C, F, heads, tl, frames_here, wide, near)),
                out_shape=jax.ShapeDtypeStruct((heads, tl, S * HD), jnp.bfloat16),
                in_specs=[pl.BlockSpec(memory_space=pl.ANY)]
                + [pl.BlockSpec(memory_space=pltpu.SMEM)] * 3,
                out_specs=pl.BlockSpec(memory_space=pltpu.VMEM),
                scratch_shapes=[
                    pltpu.VMEM((near, C, 2, 3 * rows, HD), jnp.bfloat16),
                    pltpu.VMEM((near, C, rows, HD), jnp.bfloat16),
                    pltpu.VMEM((near, rows, HD), jnp.bfloat16),
                    pltpu.VMEM((kept, S, C, 3, tl, HD), jnp.bfloat16),
                    pltpu.VMEM((heads * groups, tl, HD), jnp.bfloat16),
                    pltpu.SMEM((heads * groups,), jnp.int32),
                    dma((near, S, C)),
                    dma((near, S, C)),
                    dma((2, near, S, C)),
                    dma((heads * groups,)),
                    dma((2, near, n)),
                    dma((2, near, C)),
                    dma((2, near, n)),
                    dma((near, max(S - 1, 1))),
                    dma((heads, S, C - 1)),
                    dma((kept, S, C)),
                    dma((kept, S, C)),
                ],
                compiler_params=pltpu.CompilerParams(
                    collective_id=number, has_side_effects=True, vmem_limit_bytes=40 * 2**20
                ),
                name=f"guided_attention_{number}",
            )(ordered, timestep, windows, segments)

        return call

    operands = (ordered, timestep, windows, segments)
    wide, near = 3 * heads // 8, 3 * heads // 4
    if wide and tl * frames_here == rows:
        fits = (jnp.sum(windows > 1) <= wide * groups) & (jnp.sum(windows > 0) <= near * groups)
        out = lax.cond(fits, run(wide, near, 1), run(heads, heads, 0), *operands)
    else:
        out = run(heads, heads, 0)(*operands)
    return jnp.transpose(out, (1, 0, 2))


def solution(mesh):
    return jax.shard_map(
        body,
        mesh=mesh,
        in_specs=(P("cfg", ("groups", "frame", "seq"), None, None), P("groups"), P(), P("groups")),
        out_specs=P(("groups", "frame", "seq"), "cfg", None),
        check_vma=False,
    )
```

time: 109 us -> 84.5 us (0.78); the launches traced: 107 us -> 84.3 us
  Pallas kernels: 103 us -> 80.2 us
  other arithmetic: 0 us -> 1.29 us
  local copies, waits for them, and re-layouts: 2.86 us -> 1.57 us
    pallas_call x1 -> x2, Pallas kernels: 103 us -> 80.2 us  [the longest x1 76.1 us: call(): pl.pallas_call(functools.partial(kernel, (S, C, F, heads, tl, frames_here...]
    transpose x1 -> x0, local copies, waits for them, and re-layouts: 1.56 us -> none  [body(): return jnp.transpose(out, (1, 0, 2))]
    cond x0 -> x1, local copies, waits for them, and re-layouts: none -> 1.55 us  [body(): out = lax.cond(fits, run(wide, near, 1), run(heads, heads, 0), *operands)]
    reduce_sum x0 -> x1, other arithmetic: none -> 1.29 us  [body(): jnp.sum(windows > 0) <= near * groups]
    unnamed x4, local copies, waits for them, and re-layouts: 1.3 us -> 0.01 us
where the time goes in v2:
time: 84.5 us; the launch traced here: 84.3 us
  Pallas kernels  80.2 us (95%)
  local copies, waits for them, and re-layouts  1.57 us (2%)
  other arithmetic  1.29 us (2%)
  between operations  1.27 us (2%)
    pallas_call x1, Pallas kernels, call(): pl.pallas_call(functools.partial(kernel, (S, C, F, heads, tl, frames_here...  76.1 us
    pallas_call x1, Pallas kernels, body(): pl.pallas_call(functools.partial(gather_kernel, heads * groups, W_MAX), o...  4.03 us

profile of v2, /device:TPU:1, one launch (start us, length us, event | category | flops | bytes accessed | tf_op | source)
XLA Modules:
  0.0 84.3 jit_solution(18179209037219421111)
XLA Ops:
  0.0 1.3 %fusion.1 = (s32[]{:T(128)}, s32[]{:T(128)}) fusion(s32[32]{0:T(128)} %win_ref.1), kind=kLoop, calls=%fused_computation.4 | loop fusion | flops 190 | bytes 136 | tf_op jit(solution)/shard_map/reduce_sum | solution.py:458
  2.5 0.0 copy-start
  2.5 0.0 copy-start.1
  2.5 4.0 %order_heads.1 = bf16[32,3,256,128]{3,2,1,0:T(8,128)(2,1)S(1)} custom-call(bf16[3,256,4096]{2,1,0:T(8,128)(2,1)} %bitcast.6, s32[32]{0:T(128)} %win_ref.1), custom_call_target="tpu_custom_call" | custom-call | tf_op jit(solution)/shard_map/order_heads/pallas_call | solution.py:408
  6.6 0.0 copy-done
  6.6 0.0 copy-done.1
  6.6 76.2 %conditional.1 = (bf16[8,256,256]{2,1,0:T(8,128)(2,1)S(1)}) conditional(s32[]{:T(128)} %convert_element_type.11, (bf16[32,3,256,128]{3,2,1,0:T(8,128)(2,1)S(1)}, s32[1]{0:T(128)}, s32[32]{0:T(128)S(1)}, s32[8]{0:T(128)S(1)}) %tuple.17, (bf16[32,3,256,128]{3,2,1,0:T(8,128)(2,1)S(1)}, s32[1]{0:T(128)}, s32[32]{0:T(128)S(1)}, s32[8]{0:T(128)S(1)}) %tuple.18), branch_computations={%region_2.0_spmd, %region_3.0_spmd} | conditional | bytes 8 | solution.py:459
  6.6 76.1 %guided_attention_1.1 = bf16[8,256,256]{2,1,0:T(8,128)(2,1)S(1)} custom-call(bf16[32,3,256,128]{3,2,1,0:T(8,128)(2,1)S(1)} %get-tuple-element.28.x_ref, s32[1]{0:T(128)} %get-tuple-element.29.time_ref, s32[32]{0:T(128)S(1)} %get-tuple-element.30.win_ref, s32[8]{0:T(128)S(1)} %get-tuple-element.31.seg_ref), custom_call_target="tpu_custom_call" | custom-call | tf_op jit(solution)/shard_map/cond/branch_1_fun/guided_attention_1/pallas_call | solution.py:422
  82.8 1.6 %copy.7 = bf16[8,256,256]{2,0,1:T(8,128)(2,1)} copy(bf16[8,256,256]{2,1,0:T(8,128)(2,1)S(1)} %get-tuple-element.34) | data formatting | bytes 2097152 | tf_op jit(solution)/shard_map/cond | solution.py:459
Async XLA Ops:
  2.5 4.1 %copy-start = (s32[32]{0:T(128)S(1)}, s32[32]{0:T(128)}, u32[]{:S(2)}) copy-start(s32[32]{0:T(128)} %win_ref.1) | copy-start | bytes 388
  2.5 4.1 %copy-start.1 = (s32[8]{0:T(128)S(1)}, s32[8]{0:T(128)}, u32[]{:S(2)}) copy-start(s32[8]{0:T(128)} %param.9) | copy-start | bytes 100

commit v3 on v2

--- a/solution.py
+++ b/solution.py
@@ -15,7 +15,7 @@
 MESH = pl.DeviceIdType.MESH
 
 
-def gather_kernel(heads_all, levels, x_ref, win_ref, out_ref, sem):
+def gather_kernel(heads_all, levels, room, x_ref, win_ref, out_ref, fits_ref, sem):
     def copy(head, slot):
         return pltpu.make_async_copy(
             x_ref.at[:, :, pl.ds(pl.multiple_of(head * HD, HD), HD)], out_ref.at[slot], sem
@@ -34,8 +34,12 @@
         return step
 
     slot = jnp.int32(0)
+    fits = jnp.int32(1)
     for level in range(levels, -1, -1):
         slot = lax.fori_loop(0, heads_all, place(level), slot)
+        if level:
+            fits = fits * (slot <= room[level - 1]).astype(jnp.int32)
+    fits_ref[0] = fits
     pltpu.make_async_copy(out_ref, out_ref, sem).wait()
 
 
@@ -346,24 +350,6 @@
             def _():
                 hand_on(h - 1)
 
-    hand_on(near - 1)
-
-    @pl.loop(0, heads)
-    def _(h):
-        for s2 in range(S):
-            for dc in range(1, C):
-                r = rank(h, s2, lax.rem(c + dc, C))
-                recv(every.at[r], out_sem.at[r])
-
-    half = heads
-    for s2 in range(S):
-        for i in range(half):
-            head = s2 * (C * half) + c * half + i
-            out_ref[i, :, s2 * HD : (s2 + 1) * HD] = every[rank_ref[head]]
-
-    for lo, hi, reach in phases:
-        @pl.loop(lo, hi)
-        def _(h):
             for i, (ds, dc) in enumerate(partners):
                 send_kv(i, ds, dc, h).wait_send()
                 send_q(i, ds, dc, h).wait_send()
@@ -378,21 +364,38 @@
                     @pl.when(ok & crosses(side, s2, reach))
                     def _():
                         relay(side, i, ds, dc, h).wait_send()
-            for ds in range(1, S):
-                send_out(ds, h).wait_send()
+
+    @pl.loop(near, heads)
+    def _(h):
+        for s2 in range(S):
+            for dc in range(1, C):
+                send_local(h, s2, dc).wait_send()
+
+    hand_on(near - 1)
 
     @pl.loop(0, heads)
     def _(h):
         for s2 in range(S):
             for dc in range(1, C):
+                r = rank(h, s2, lax.rem(c + dc, C))
+                recv(every.at[r], out_sem.at[r])
+
+    half = heads
+    for s2 in range(S):
+        for i in range(half):
+            head = s2 * (C * half) + c * half + i
+            out_ref[i, :, s2 * HD : (s2 + 1) * HD] = every[rank_ref[head]]
+
+    @pl.loop(0, near)
+    def _(h):
+        for ds in range(1, S):
+            send_out(ds, h).wait_send()
+
+    @pl.loop(0, heads)
+    def _(h):
+        for s2 in range(S):
+            for dc in range(1, C):
                 send_core(h, s2, dc, every.at[rank(h, s2, c)]).wait_send()
-
-    @pl.loop(near, heads)
-    def _(h):
-        for s2 in range(S):
-            for dc in range(1, C):
-                send_local(h, s2, dc).wait_send()
-
 
 def body(qkv, timestep, windows, segments):
     S, C, F = (lax.axis_size(axis) for axis in ("seq", "cfg", "frame"))
@@ -405,11 +408,19 @@
     groups = S * C
     n = groups - 1
     dma = pltpu.SemaphoreType.DMA
-    ordered = pl.pallas_call(
-        functools.partial(gather_kernel, heads * groups, W_MAX),
-        out_shape=jax.ShapeDtypeStruct((heads * groups, 3, tl, HD), x.dtype),
+    wide, near = 3 * heads // 8, 3 * heads // 4
+    room = (near * groups,) * (W_MAX - 1) + (wide * groups,)
+    ordered, fits = pl.pallas_call(
+        functools.partial(gather_kernel, heads * groups, W_MAX, room),
+        out_shape=(
+            jax.ShapeDtypeStruct((heads * groups, 3, tl, HD), x.dtype),
+            jax.ShapeDtypeStruct((1,), jnp.int32),
+        ),
         in_specs=[pl.BlockSpec(memory_space=pl.ANY), pl.BlockSpec(memory_space=pltpu.SMEM)],
-        out_specs=pl.BlockSpec(memory_space=pltpu.VMEM),
+        out_specs=(
+            pl.BlockSpec(memory_space=pltpu.VMEM),
+            pl.BlockSpec(memory_space=pltpu.SMEM),
+        ),
         scratch_shapes=[dma],
         name="order_heads",
         compiler_params=pltpu.CompilerParams(vmem_limit_bytes=56 * 2**20),
@@ -453,10 +464,8 @@
         return call
 
     operands = (ordered, timestep, windows, segments)
-    wide, near = 3 * heads // 8, 3 * heads // 4
     if wide and tl * frames_here == rows:
-        fits = (jnp.sum(windows > 1) <= wide * groups) & (jnp.sum(windows > 0) <= near * groups)
-        out = lax.cond(fits, run(wide, near, 1), run(heads, heads, 0), *operands)
+        out = lax.cond(fits[0] > 0, run(wide, near, 1), run(heads, heads, 0), *operands)
     else:
         out = run(heads, heads, 0)(*operands)
     return jnp.transpose(out, (1, 0, 2))

time: 84.5 us -> 83.1 us (0.983)
  other arithmetic: 1.29 us -> 0 us
    reduce_sum x1 -> x0, other arithmetic: 1.29 us -> none  [body(): jnp.sum(windows > 0) <= near * groups]
where the time goes in v3:
time: 83.1 us; the launch traced here: 82.9 us
  Pallas kernels  80.6 us (97%)
  local copies, waits for them, and re-layouts  1.56 us (2%)
    pallas_call x1, Pallas kernels, call(): pl.pallas_call(functools.partial(kernel, (S, C, F, heads, tl, frames_here...  76.1 us
    pallas_call x1, Pallas kernels, body(): pl.pallas_call(functools.partial(gather_kernel, heads * groups, W_MAX, ro...  4.54 us

profile of v3, /device:TPU:1, one launch (start us, length us, event | category | flops | bytes accessed | tf_op | source)
XLA Modules:
  0.0 82.9 jit_solution(6323630571189166683)
XLA Ops:
  0.0 0.0 copy-start
  0.0 0.0 copy-start.1
  0.0 4.5 %order_heads.1 = (bf16[32,3,256,128]{3,2,1,0:T(8,128)(2,1)S(1)}, s32[1]{0:T(128)}) custom-call(bf16[3,256,4096]{2,1,0:T(8,128)(2,1)} %bitcast.7, s32[32]{0:T(128)} %win_ref.1), custom_call_target="tpu_custom_call" | custom-call | tf_op jit(solution)/shard_map/order_heads/pallas_call | solution.py:413
  5.2 0.0 copy-done
  5.2 0.0 copy-done.1
  5.2 76.1 %conditional.1 = (bf16[8,256,256]{2,1,0:T(8,128)(2,1)S(1)}) conditional(s32[]{:T(128)} %bitcast.2, (bf16[32,3,256,128]{3,2,1,0:T(8,128)(2,1)S(1)}, s32[1]{0:T(128)}, s32[32]{0:T(128)S(1)}, s32[8]{0:T(128)S(1)}) %tuple.16, (bf16[32,3,256,128]{3,2,1,0:T(8,128)(2,1)S(1)}, s32[1]{0:T(128)}, s32[32]{0:T(128)S(1)}, s32[8]{0:T(128)S(1)}) %tuple.17), branch_computations={%region_0.0_spmd, %region_1.0_spmd} | conditional | bytes 8 | solution.py:468
  5.2 76.1 %guided_attention_1.1 = bf16[8,256,256]{2,1,0:T(8,128)(2,1)S(1)} custom-call(bf16[32,3,256,128]{3,2,1,0:T(8,128)(2,1)S(1)} %get-tuple-element.28.x_ref, s32[1]{0:T(128)} %get-tuple-element.29.time_ref, s32[32]{0:T(128)S(1)} %get-tuple-element.30.win_ref, s32[8]{0:T(128)S(1)} %get-tuple-element.31.seg_ref), custom_call_target="tpu_custom_call" | custom-call | tf_op jit(solution)/shard_map/cond/branch_1_fun/guided_attention_1/pallas_call | solution.py:433
  81.3 1.6 %copy.7 = bf16[8,256,256]{2,0,1:T(8,128)(2,1)} copy(bf16[8,256,256]{2,1,0:T(8,128)(2,1)S(1)} %get-tuple-element.36) | data formatting | bytes 2097152 | tf_op jit(solution)/shard_map/cond | solution.py:468
Async XLA Ops:
  0.0 5.2 %copy-start = (s32[32]{0:T(128)S(1)}, s32[32]{0:T(128)}, u32[]{:S(2)}) copy-start(s32[32]{0:T(128)} %win_ref.1) | copy-start | bytes 388
  0.0 5.2 %copy-start.1 = (s32[8]{0:T(128)S(1)}, s32[8]{0:T(128)}, u32[]{:S(2)}) copy-start(s32[8]{0:T(128)} %param.9) | copy-start | bytes 100

commit v4 on v3

--- a/solution.py
+++ b/solution.py
@@ -49,7 +49,7 @@
     kv_sem, q_sem, halo_sem, out_sem, a2a_send, own_send, relay_send, out_send, core_send,
     l_sem, l_send,
 ):
-    S, C, F, heads, tl, frames_here, wide, near = dims
+    S, C, F, heads, tl, frames_here, wide, near, short = dims
     groups = S * C
     rows = S * tl
     per_frame = rows // frames_here
@@ -66,10 +66,18 @@
         return lax.rem(s + ds, S), lax.rem(c + dc, C)
 
     def rank(h, s2, c2):
-        return h * groups + s2 * C + c2
+        return h * groups + c2 * S + s2
 
     def token_rows(base, piece):
         return pl.ds(pl.multiple_of(base + piece * tl, tl), tl)
+
+    def full(core):
+        return wide - jnp.where(core > 0, short, 0)
+
+    def shared(core):
+        return near - jnp.where(core > 0, short, 0)
+
+    low = near - short
 
     barrier = pltpu.get_barrier_semaphore()
     for ds, dc in partners:
@@ -147,10 +155,8 @@
             device_id={"frame": neighbour(side)}, device_id_type=MESH,
         )
 
-    def crosses(side, s2, reach):
-        if reach == W_MAX:
-            return s2 >= 0
-        return s2 == (S - 1 if side == 0 else 0)
+    def crosses(side, s2, h, core):
+        return (h < full(core)) | (s2 == (S - 1 if side == 0 else 0))
 
     def send_out(ds, h):
         s2 = lax.rem(s + ds, S)
@@ -175,15 +181,15 @@
         c2 = lax.rem(c + dc, C)
         return pltpu.make_async_remote_copy(
             src_ref=x_ref.at[rank(h, s2, c2)],
-            dst_ref=lb.at[h - near, s2, c],
-            send_sem=l_send.at[h - near, s2, dc],
-            recv_sem=l_sem.at[h - near, s2, c],
+            dst_ref=lb.at[h - low, s2, c],
+            send_sem=l_send.at[h - low, s2, dc],
+            recv_sem=l_sem.at[h - low, s2, c],
             device_id={"cfg": c2}, device_id_type=MESH,
         )
 
     def own_local(h, s2):
         return pltpu.make_async_copy(
-            x_ref.at[rank(h, s2, c)], lb.at[h - near, s2, c], l_sem.at[h - near, s2, c]
+            x_ref.at[rank(h, s2, c)], lb.at[h - low, s2, c], l_sem.at[h - low, s2, c]
         )
 
     def recv(ref, sem):
@@ -192,33 +198,62 @@
             device_id={"seq": s}, device_id_type=MESH,
         ).wait_recv()
 
-    phases = ((0, wide, W_MAX), (wide, near, 1))
     sides = ((0, up_ok), (1, down_ok))
 
-    for lo, hi, reach in phases:
-        @pl.loop(lo, hi)
+    def each_partner(h, act):
+        for i, (ds, dc) in enumerate(partners):
+            @pl.when(h < shared(lax.rem(c + dc, C)))
+            def _():
+                act(i, ds, dc, h)
+
+    def each_halo(h, act):
+        for side, ok in sides:
+            for dc in range(C):
+                c2 = lax.rem(c + dc, C)
+
+                @pl.when(ok & (h < shared(c2)) & crosses(side, s, h, c2))
+                def _():
+                    act(send_halo(side, dc, h))
+
+    def each_relay(i, ds, dc, h, act):
+        s2, b = at(ds, dc)
+        for side, ok in sides:
+            @pl.when(ok & crosses(side, s2, h, c))
+            def _():
+                act(relay(side, i, ds, dc, h))
+
+    def each_local(act):
+        @pl.loop(low, heads)
         def _(h):
-            for i, (ds, dc) in enumerate(partners):
-                send_kv(i, ds, dc, h).start()
-            for side, ok in sides:
-                @pl.when(ok & crosses(side, s, reach))
-                def _():
-                    for dc in range(C):
-                        send_halo(side, dc, h).start()
+            for s2 in range(S):
+                for dc in range(1, C):
+                    @pl.when(h >= shared(lax.rem(c + dc, C)))
+                    def _():
+                        act(send_local(h, s2, dc))
+
+    @pl.loop(0, near)
+    def _(h):
+        each_partner(h, lambda *k: send_kv(*k).start())
+        each_halo(h, lambda copy: copy.start())
+
+        @pl.when(h < shared(c))
+        def _():
             own_kv(h).start()
 
-    @pl.loop(near, heads)
+    each_local(lambda copy: copy.start())
+
+    @pl.loop(shared(c), heads)
     def _(h):
         for s2 in range(S):
-            for dc in range(1, C):
-                send_local(h, s2, dc).start()
             own_local(h, s2).start()
 
     @pl.loop(0, near)
     def _(h):
-        for i, (ds, dc) in enumerate(partners):
-            send_q(i, ds, dc, h).start()
-        own_q(h).start()
+        each_partner(h, lambda *k: send_q(*k).start())
+
+        @pl.when(h < shared(c))
+        def _():
+            own_q(h).start()
 
     for edge, base in ((f == 0, 0), (f == F - 1, 2 * rows)):
         @pl.when(edge)
@@ -259,31 +294,27 @@
     def guide(cond, uncond):
         return (uncond + strength * (cond - uncond)).astype(jnp.bfloat16)
 
-    @pl.loop(near, heads)
+    @pl.loop(shared(c), heads)
     def _(h):
         for s2 in range(S):
             own_local(h, s2).wait()
             for dc in range(1, C):
                 b = lax.rem(c + dc, C)
-                recv(lb.at[h - near, s2, b], l_sem.at[h - near, s2, b])
+                recv(lb.at[h - low, s2, b], l_sem.at[h - low, s2, b])
             cond, uncond = [
-                attend(lb[h - near, s2, b, 0], lb[h - near, s2, b, 1], lb[h - near, s2, b, 2], None)
+                attend(lb[h - low, s2, b, 0], lb[h - low, s2, b, 1], lb[h - low, s2, b, 2], None)
                 for b in range(C)
             ]
             every[rank(h, s2, c)] = guide(cond, uncond)
             for dc in range(1, C):
                 send_core(h, s2, dc, every.at[rank(h, s2, c)]).start()
 
-    for lo, hi, reach in phases:
-        @pl.loop(lo, hi)
-        def _(h):
-            for i, ds, dc in others:
-                s2, b = at(ds, dc)
-                recv(kv.at[h, b, :, token_rows(rows, s2), :], kv_sem.at[h, s2, b])
-                for side, ok in sides:
-                    @pl.when(ok & crosses(side, s2, reach))
-                    def _():
-                        relay(side, i, ds, dc, h).start()
+    @pl.loop(0, shared(c))
+    def _(h):
+        for i, ds, dc in others:
+            s2, b = at(ds, dc)
+            recv(kv.at[h, b, :, token_rows(rows, s2), :], kv_sem.at[h, s2, b])
+            each_relay(i, ds, dc, h, lambda copy: copy.start())
 
     def hand_on(h):
         for ds in range(1, S):
@@ -293,7 +324,7 @@
             for dc in range(1, C):
                 send_core(h, s2, dc, ref).start()
 
-    for lo, hi, reach in phases:
+    for lo, hi, reach in ((0, full(c), W_MAX), (full(c), shared(c), 1)):
         @pl.loop(lo, hi)
         def _(h):
             own_kv(h).wait()
@@ -307,7 +338,7 @@
                 for ds in range(S):
                     s2 = lax.rem(s + ds, S)
 
-                    @pl.when(ok & crosses(side, s2, reach))
+                    @pl.when(ok & crosses(side, s2, h, c))
                     def _():
                         for b in range(C):
                             recv(
@@ -350,28 +381,20 @@
             def _():
                 hand_on(h - 1)
 
-            for i, (ds, dc) in enumerate(partners):
-                send_kv(i, ds, dc, h).wait_send()
-                send_q(i, ds, dc, h).wait_send()
-            for side, ok in sides:
-                @pl.when(ok & crosses(side, s, reach))
-                def _():
-                    for dc in range(C):
-                        send_halo(side, dc, h).wait_send()
-                for i, ds, dc in others:
-                    s2, b = at(ds, dc)
-
-                    @pl.when(ok & crosses(side, s2, reach))
-                    def _():
-                        relay(side, i, ds, dc, h).wait_send()
-
-    @pl.loop(near, heads)
-    def _(h):
-        for s2 in range(S):
-            for dc in range(1, C):
-                send_local(h, s2, dc).wait_send()
-
-    hand_on(near - 1)
+    hand_on(shared(c) - 1)
+
+    @pl.loop(0, near)
+    def _(h):
+        each_partner(h, lambda *k: send_kv(*k).wait_send())
+        each_partner(h, lambda *k: send_q(*k).wait_send())
+        each_halo(h, lambda copy: copy.wait_send())
+
+    @pl.loop(0, shared(c))
+    def _(h):
+        for i, ds, dc in others:
+            each_relay(i, ds, dc, h, lambda copy: copy.wait_send())
+
+    each_local(lambda copy: copy.wait_send())
 
     @pl.loop(0, heads)
     def _(h):
@@ -386,7 +409,7 @@
             head = s2 * (C * half) + c * half + i
             out_ref[i, :, s2 * HD : (s2 + 1) * HD] = every[rank_ref[head]]
 
-    @pl.loop(0, near)
+    @pl.loop(0, shared(c))
     def _(h):
         for ds in range(1, S):
             send_out(ds, h).wait_send()
@@ -409,7 +432,9 @@
     n = groups - 1
     dma = pltpu.SemaphoreType.DMA
     wide, near = 3 * heads // 8, 3 * heads // 4
-    room = (near * groups,) * (W_MAX - 1) + (wide * groups,)
+    short = 1 if heads > 4 else 0
+    cut = short * S * (C - 1)
+    room = (near * groups - cut,) * (W_MAX - 1) + (wide * groups - cut,)
     ordered, fits = pl.pallas_call(
         functools.partial(gather_kernel, heads * groups, W_MAX, room),
         out_shape=(
@@ -426,12 +451,12 @@
         compiler_params=pltpu.CompilerParams(vmem_limit_bytes=56 * 2**20),
     )(x, windows)
 
-    def run(wide, near, number):
-        kept = max(heads - near, 1)
+    def run(wide, near, short, number):
+        kept = max(heads - near + short, 1)
 
         def call(ordered, timestep, windows, segments):
             return pl.pallas_call(
-                functools.partial(kernel, (S, C, F, heads, tl, frames_here, wide, near)),
+                functools.partial(kernel, (S, C, F, heads, tl, frames_here, wide, near, short)),
                 out_shape=jax.ShapeDtypeStruct((heads, tl, S * HD), jnp.bfloat16),
                 in_specs=[pl.BlockSpec(memory_space=pl.ANY)]
                 + [pl.BlockSpec(memory_space=pltpu.SMEM)] * 3,
@@ -465,9 +490,9 @@
 
     operands = (ordered, timestep, windows, segments)
     if wide and tl * frames_here == rows:
-        out = lax.cond(fits[0] > 0, run(wide, near, 1), run(heads, heads, 0), *operands)
+        out = lax.cond(fits[0] > 0, run(wide, near, short, 1), run(heads, heads, 0, 0), *operands)
     else:
-        out = run(heads, heads, 0)(*operands)
+        out = run(heads, heads, 0, 0)(*operands)
     return jnp.transpose(out, (1, 0, 2))
 
 

time: 83.1 us -> 78.4 us (0.943)
  Pallas kernels: 80.6 us -> 75.9 us
    pallas_call x1, Pallas kernels: 76.1 us -> 71.4 us  [call(): pl.pallas_call(functools.partial(kernel, (S, C, F, heads, tl, frames_here...]
where the time goes in v4:
time: 78.4 us; the launch traced here: 78.2 us
  Pallas kernels  75.9 us (97%)
  local copies, waits for them, and re-layouts  1.56 us (2%)
    pallas_call x1, Pallas kernels, call(): pl.pallas_call(functools.partial(kernel, (S, C, F, heads, tl, frames_here...  71.4 us
    pallas_call x1, Pallas kernels, body(): pl.pallas_call(functools.partial(gather_kernel, heads * groups, W_MAX, ro...  4.54 us

profile of v4, /device:TPU:1, one launch (start us, length us, event | category | flops | bytes accessed | tf_op | source)
XLA Modules:
  0.0 78.2 jit_solution(17652577102022627585)
XLA Ops:
  0.0 0.0 copy-start
  0.0 0.0 copy-start.1
  0.0 4.5 %order_heads.1 = (bf16[32,3,256,128]{3,2,1,0:T(8,128)(2,1)S(1)}, s32[1]{0:T(128)}) custom-call(bf16[3,256,4096]{2,1,0:T(8,128)(2,1)} %bitcast.7, s32[32]{0:T(128)} %win_ref.1), custom_call_target="tpu_custom_call" | custom-call | tf_op jit(solution)/shard_map/order_heads/pallas_call | solution.py:438
  5.2 0.0 copy-done
  5.2 0.0 copy-done.1
  5.2 71.4 %conditional.1 = (bf16[8,256,256]{2,1,0:T(8,128)(2,1)S(1)}) conditional(s32[]{:T(128)} %bitcast.2, (bf16[32,3,256,128]{3,2,1,0:T(8,128)(2,1)S(1)}, s32[1]{0:T(128)}, s32[32]{0:T(128)S(1)}, s32[8]{0:T(128)S(1)}) %tuple.16, (bf16[32,3,256,128]{3,2,1,0:T(8,128)(2,1)S(1)}, s32[1]{0:T(128)}, s32[32]{0:T(128)S(1)}, s32[8]{0:T(128)S(1)}) %tuple.17), branch_computations={%region_0.0_spmd, %region_1.0_spmd} | conditional | bytes 8 | solution.py:493
  5.2 71.4 %guided_attention_1.1 = bf16[8,256,256]{2,1,0:T(8,128)(2,1)S(1)} custom-call(bf16[32,3,256,128]{3,2,1,0:T(8,128)(2,1)S(1)} %get-tuple-element.28.x_ref, s32[1]{0:T(128)} %get-tuple-element.29.time_ref, s32[32]{0:T(128)S(1)} %get-tuple-element.30.win_ref, s32[8]{0:T(128)S(1)} %get-tuple-element.31.seg_ref), custom_call_target="tpu_custom_call" | custom-call | tf_op jit(solution)/shard_map/cond/branch_1_fun/guided_attention_1/pallas_call | solution.py:458
  76.6 1.6 %copy.7 = bf16[8,256,256]{2,0,1:T(8,128)(2,1)} copy(bf16[8,256,256]{2,1,0:T(8,128)(2,1)S(1)} %get-tuple-element.36) | data formatting | bytes 2097152 | tf_op jit(solution)/shard_map/cond | solution.py:493
Async XLA Ops:
  0.0 5.2 %copy-start = (s32[32]{0:T(128)S(1)}, s32[32]{0:T(128)}, u32[]{:S(2)}) copy-start(s32[32]{0:T(128)} %win_ref.1) | copy-start | bytes 388
  0.0 5.2 %copy-start.1 = (s32[8]{0:T(128)S(1)}, s32[8]{0:T(128)}, u32[]{:S(2)}) copy-start(s32[8]{0:T(128)} %param.9) | copy-start | bytes 100
